TPU v7x, 32 devices: a whole 2x2x4 slice. The times are simulated.
32 devices in a mesh: row: 8 (over y, x, core), col: 4 (over z).
Axes of the slice: x: 2, y: 2, z: 4, core: 2. Of those that a mesh axis runs over, the one named last changes fastest.
Arguments:
- left_panels: float32 [8, 4, 16, 128, 128], P('row', 'col'), may hold values from -6 to 6
- right_panels: float32 [2, 4, 8, 12, 128, 128], P(None, 'col', 'row'), may hold values from -0.25 to 0.25
- product_lists: int32 [8, 4, 8, 96, 3], P('row', 'col'), may hold values from -1 to 23, as said below
Outputs:
- product_blocks: float32 [8, 4, 24, 128, 128], P('row', 'col')
Inputs may be any that keep to these rules, and one draw needn't show every extreme that they name: `product_lists`: each entry is (left slot < 16, right slot < 12, output slot < 24). In each list the first entries, at least half of 96 and at most 96, are live with distinct (left, right) pairs, the rest are -1 in all three columns; some list holds 96 live entries.
All inputs are finite; a program needn't handle non-finite values.
Results may differ from a plain program's by a relative error of at most 0.0003.
Values sent between devices are 32-bit elements; how exact they have to be, the bound alone decides.
A program may use at most 128 MiB of HBM per device.

v0:
```python
import jax
import jax.numpy as jnp
from jax import lax
from jax.sharding import PartitionSpec as P

BLK = 128
OCAP = 24


def contribute(left_stack, right_panel, entries, slot_count):
    live_mask = entries[:, 0] >= 0
    left_slot = jnp.maximum(entries[:, 0], 0)
    right_slot = jnp.maximum(entries[:, 1], 0)
    taken_left = jnp.take(left_stack, left_slot, axis=0)
    taken_right = jnp.take(right_panel, right_slot, axis=0)
    blocks = jnp.einsum("pik,pkj->pij", taken_left, taken_right, precision=lax.Precision.HIGHEST)
    slot_ids = jnp.arange(slot_count, dtype=jnp.int32)
    onehot = ((entries[:, 2][None, :] == slot_ids[:, None]) & live_mask[None, :]).astype(
        blocks.dtype
    )
    return jnp.einsum("op,pij->oij", onehot, blocks, precision=lax.Precision.HIGHEST)


def shards(left_panels, right_panels, product_lists):
    row_count = lax.axis_size("row")
    col_count = lax.axis_size("col")
    row_pos = lax.axis_index("row")
    col_pos = lax.axis_index("col")
    entries = product_lists[0, 0]
    step_count = entries.shape[0]
    running = jnp.zeros((OCAP, BLK, BLK), jnp.float32)
    right_all = lax.all_gather(right_panels, "col", axis=1, tiled=True)
    pieces = lax.all_gather(left_panels, "row", axis=0, tiled=True)

    def one_row(offset, partial_value):
        step_num = (offset - row_pos - col_pos) % row_count
        left_stack = lax.dynamic_index_in_dim(pieces, offset, 0, keepdims=False)[0]
        right_panel = right_all[offset // col_count, offset % col_count, 0]
        entry_rows = lax.dynamic_index_in_dim(
            entries, jnp.minimum(step_num, step_count - 1), 0, keepdims=False
        )
        return lax.cond(
            step_num < step_count,
            lambda inner: inner + contribute(left_stack, right_panel, entry_rows, OCAP),
            lambda inner: inner,
            partial_value,
        )

    running = lax.fori_loop(0, pieces.shape[0], one_row, running)
    return running[None, None]


def solution(mesh):
    return jax.shard_map(
        shards,
        mesh=mesh,
        in_specs=(
            P("row", "col", None, None, None),
            P(None, "col", "row", None, None, None),
            P("row", "col", None, None, None),
        ),
        out_specs=P("row", "col", None, None, None),
        check_vma=False,
    )
```

profile of v0, /device:TPU:0, one launch (start us, length us, event | category | flops | bytes accessed | tf_op | source)
XLA Modules:
  0.0 394.5 jit_solution(15243626719083775768)
XLA Ops:
  6.5 0.7 all-gather.5.cloned.1.call-update
  7.3 0.7 all-gather.3.cloned.1.call-update
  8.0 0.7 copy.16
  8.7 118.3 %all-gather.5.cloned.1.call-done = f32[2,4,1,12,128,128]{5,4,3,2,1,0:T(8,128)} async-done(((f32[2,1,1,12,128,128]{5,4,3,2,1,0:T(8,128)}), f32[2,4,1,12,128,128]{5,4,3,2,1,0:T(8,128)}) %all-gather.5.cloned.1.call-update) | async-done | bytes 6291472 | tf_op jit(solution)/shard_map/all_gather | solution.py:32
  127.0 54.4 %all-gather.3.cloned.1.call-done = f32[8,1,16,128,128]{4,3,2,1,0:T(8,128)} async-done(((f32[1,1,16,128,128]{4,3,2,1,0:T(8,128)}), f32[8,1,16,128,128]{4,3,2,1,0:T(8,128)}) %all-gather.3.cloned.1.call-update) | async-done | bytes 8388624 | tf_op jit(solution)/shard_map/all_gather | solution.py:33
  181.3 0.1 broadcast_in_dim.38
  181.5 204.8 %while.19 = (s32[]{:T(128)}, f32[24,128,128]{2,0,1:T(8,128)S(1)}, s32[]{:T(128)}, s32[]{:T(128)}, s32[8,96,3]{1,2,0:T(4,128)S(1)}, /*index=5*/f32[8,1,16,128,128...) while((s32[]{:T(128)}, f32[24,128,128]{2,0,1:T(8,128)S(1)}, ...), condition=%wide.region_3.4_spmd, body=%wide.region_0.3_spmd.sunk | while | flops 2872450304 | bytes 57164012 | solution.py:49
  181.5 25.6 %conditional.2 = (f32[24,128,128]{2,0,1:T(8,128)S(1)}) conditional(s32[]{:T(128)} %convert_element_type.13, f32[24,128,128]{2,0,1:T(8,128)S(1)} %get-tuple-element.574, (s32[]{:T(128)}, s32[8,96,3]{1,2,0:T(4,128)S(1)}, s32[]{:T(128)}, f32[8,1,16,128,128]{4,3,2,1,0:T(8,128)}, f32[2,4,1,12,128,128]{5,4,3,2,1,0:T(8,128)}, ...), branch_computations={%region_1.1_spmd, %region_2.2_spmd} | conditional | flops 2872450304 | bytes 57163708 | solution.py:42
  181.5 1.2 dynamic-slice_bitcast_fusion.1
  182.8 3.5 gather_fusion.1
  186.3 1.3 dynamic-slice_bitcast_fusion
  187.6 3.6 gather_fusion
  191.2 9.5 %fusion.2 = f32[96,128,128]{2,1,0:T(8,128)S(1)} fusion(f32[96,128,128]{2,1,0:T(8,128)} %gather_fusion.1, f32[96,128,128]{2,1,0:T(8,128)} %gather_fusion, pred[96]{0:T(512)(128)(4,1)S(1)} %get-tuple-element.513, pred[96]{0:T(512)(128)(4,1)S(1)} %get-tuple-element.512), kind=kOutput, calls=%fused_computation.4 | convolution fusion | flops 2419064832 | bytes 18874560 | tf_op jit(solution)/shard_map/while/body/eval_jaxpr/cond/branch_1_fun/pik,pkj->pij/dot_general | solution.py:16
  200.8 6.3 %fusion.8 = f32[24,128,128]{2,0,1:T(8,128)S(1)} fusion(f32[24,128,128]{2,0,1:T(8,128)S(1)} %get-tuple-element.481, f32[96,128,128]{2,1,0:T(8,128)S(1)} %fusion.2, s32[96]{0:T(128)S(1)} %get-tuple-element.514, pred[96]{0:T(512)(128)(4,1)S(1)} %get-tuple-element.511), kind=kOutput, calls=%fused_computation.10 | convolution fusion | flops 453382656 | bytes 9437664 | tf_op jit(solution)/shard_map/while/body/eval_jaxpr/cond/branch_1_fun/op,pij->oij/dot_general | solution.py:21
  207.1 25.6 %conditional.2 = (f32[24,128,128]{2,0,1:T(8,128)S(1)}) conditional(s32[]{:T(128)} %convert_element_type.13, f32[24,128,128]{2,0,1:T(8,128)S(1)} %get-tuple-element.574, (s32[]{:T(128)}, s32[8,96,3]{1,2,0:T(4,128)S(1)}, s32[]{:T(128)}, f32[8,1,16,128,128]{4,3,2,1,0:T(8,128)}, f32[2,4,1,12,128,128]{5,4,3,2,1,0:T(8,128)}, ...), branch_computations={%region_1.1_spmd, %region_2.2_spmd} | conditional | flops 2872450304 | bytes 57163708 | solution.py:42
  207.1 1.2 dynamic-slice_bitcast_fusion.1
  208.4 3.5 gather_fusion.1
  211.9 1.3 dynamic-slice_bitcast_fusion
  213.2 3.6 gather_fusion
  216.8 9.5 %fusion.2 = f32[96,128,128]{2,1,0:T(8,128)S(1)} fusion(f32[96,128,128]{2,1,0:T(8,128)} %gather_fusion.1, f32[96,128,128]{2,1,0:T(8,128)} %gather_fusion, pred[96]{0:T(512)(128)(4,1)S(1)} %get-tuple-element.513, pred[96]{0:T(512)(128)(4,1)S(1)} %get-tuple-element.512), kind=kOutput, calls=%fused_computation.4 | convolution fusion | flops 2419064832 | bytes 18874560 | tf_op jit(solution)/shard_map/while/body/eval_jaxpr/cond/branch_1_fun/pik,pkj->pij/dot_general | solution.py:16
  226.4 6.3 %fusion.8 = f32[24,128,128]{2,0,1:T(8,128)S(1)} fusion(f32[24,128,128]{2,0,1:T(8,128)S(1)} %get-tuple-element.481, f32[96,128,128]{2,1,0:T(8,128)S(1)} %fusion.2, s32[96]{0:T(128)S(1)} %get-tuple-element.514, pred[96]{0:T(512)(128)(4,1)S(1)} %get-tuple-element.511), kind=kOutput, calls=%fused_computation.10 | convolution fusion | flops 453382656 | bytes 9437664 | tf_op jit(solution)/shard_map/while/body/eval_jaxpr/cond/branch_1_fun/op,pij->oij/dot_general | solution.py:21
  232.7 25.6 %conditional.2 = (f32[24,128,128]{2,0,1:T(8,128)S(1)}) conditional(s32[]{:T(128)} %convert_element_type.13, f32[24,128,128]{2,0,1:T(8,128)S(1)} %get-tuple-element.574, (s32[]{:T(128)}, s32[8,96,3]{1,2,0:T(4,128)S(1)}, s32[]{:T(128)}, f32[8,1,16,128,128]{4,3,2,1,0:T(8,128)}, f32[2,4,1,12,128,128]{5,4,3,2,1,0:T(8,128)}, ...), branch_computations={%region_1.1_spmd, %region_2.2_spmd} | conditional | flops 2872450304 | bytes 57163708 | solution.py:42
  232.7 1.2 dynamic-slice_bitcast_fusion.1
  234.0 3.5 gather_fusion.1
  237.5 1.3 dynamic-slice_bitcast_fusion
  238.8 3.6 gather_fusion
  242.4 9.5 %fusion.2 = f32[96,128,128]{2,1,0:T(8,128)S(1)} fusion(f32[96,128,128]{2,1,0:T(8,128)} %gather_fusion.1, f32[96,128,128]{2,1,0:T(8,128)} %gather_fusion, pred[96]{0:T(512)(128)(4,1)S(1)} %get-tuple-element.513, pred[96]{0:T(512)(128)(4,1)S(1)} %get-tuple-element.512), kind=kOutput, calls=%fused_computation.4 | convolution fusion | flops 2419064832 | bytes 18874560 | tf_op jit(solution)/shard_map/while/body/eval_jaxpr/cond/branch_1_fun/pik,pkj->pij/dot_general | solution.py:16
  252.0 6.3 %fusion.8 = f32[24,128,128]{2,0,1:T(8,128)S(1)} fusion(f32[24,128,128]{2,0,1:T(8,128)S(1)} %get-tuple-element.481, f32[96,128,128]{2,1,0:T(8,128)S(1)} %fusion.2, s32[96]{0:T(128)S(1)} %get-tuple-element.514, pred[96]{0:T(512)(128)(4,1)S(1)} %get-tuple-element.511), kind=kOutput, calls=%fused_computation.10 | convolution fusion | flops 453382656 | bytes 9437664 | tf_op jit(solution)/shard_map/while/body/eval_jaxpr/cond/branch_1_fun/op,pij->oij/dot_general | solution.py:21
  258.3 25.6 %conditional.2 = (f32[24,128,128]{2,0,1:T(8,128)S(1)}) conditional(s32[]{:T(128)} %convert_element_type.13, f32[24,128,128]{2,0,1:T(8,128)S(1)} %get-tuple-element.574, (s32[]{:T(128)}, s32[8,96,3]{1,2,0:T(4,128)S(1)}, s32[]{:T(128)}, f32[8,1,16,128,128]{4,3,2,1,0:T(8,128)}, f32[2,4,1,12,128,128]{5,4,3,2,1,0:T(8,128)}, ...), branch_computations={%region_1.1_spmd, %region_2.2_spmd} | conditional | flops 2872450304 | bytes 57163708 | solution.py:42
  258.3 1.2 dynamic-slice_bitcast_fusion.1
  259.6 3.5 gather_fusion.1
  263.1 1.3 dynamic-slice_bitcast_fusion
  264.4 3.6 gather_fusion
  268.0 9.5 %fusion.2 = f32[96,128,128]{2,1,0:T(8,128)S(1)} fusion(f32[96,128,128]{2,1,0:T(8,128)} %gather_fusion.1, f32[96,128,128]{2,1,0:T(8,128)} %gather_fusion, pred[96]{0:T(512)(128)(4,1)S(1)} %get-tuple-element.513, pred[96]{0:T(512)(128)(4,1)S(1)} %get-tuple-element.512), kind=kOutput, calls=%fused_computation.4 | convolution fusion | flops 2419064832 | bytes 18874560 | tf_op jit(solution)/shard_map/while/body/eval_jaxpr/cond/branch_1_fun/pik,pkj->pij/dot_general | solution.py:16
  277.6 6.3 %fusion.8 = f32[24,128,128]{2,0,1:T(8,128)S(1)} fusion(f32[24,128,128]{2,0,1:T(8,128)S(1)} %get-tuple-element.481, f32[96,128,128]{2,1,0:T(8,128)S(1)} %fusion.2, s32[96]{0:T(128)S(1)} %get-tuple-element.514, pred[96]{0:T(512)(128)(4,1)S(1)} %get-tuple-element.511), kind=kOutput, calls=%fused_computation.10 | convolution fusion | flops 453382656 | bytes 9437664 | tf_op jit(solution)/shard_map/while/body/eval_jaxpr/cond/branch_1_fun/op,pij->oij/dot_general | solution.py:21
  283.9 25.6 %conditional.2 = (f32[24,128,128]{2,0,1:T(8,128)S(1)}) conditional(s32[]{:T(128)} %convert_element_type.13, f32[24,128,128]{2,0,1:T(8,128)S(1)} %get-tuple-element.574, (s32[]{:T(128)}, s32[8,96,3]{1,2,0:T(4,128)S(1)}, s32[]{:T(128)}, f32[8,1,16,128,128]{4,3,2,1,0:T(8,128)}, f32[2,4,1,12,128,128]{5,4,3,2,1,0:T(8,128)}, ...), branch_computations={%region_1.1_spmd, %region_2.2_spmd} | conditional | flops 2872450304 | bytes 57163708 | solution.py:42
  283.9 1.2 dynamic-slice_bitcast_fusion.1
  285.2 3.5 gather_fusion.1
  288.7 1.3 dynamic-slice_bitcast_fusion
  290.0 3.6 gather_fusion
  293.6 9.5 %fusion.2 = f32[96,128,128]{2,1,0:T(8,128)S(1)} fusion(f32[96,128,128]{2,1,0:T(8,128)} %gather_fusion.1, f32[96,128,128]{2,1,0:T(8,128)} %gather_fusion, pred[96]{0:T(512)(128)(4,1)S(1)} %get-tuple-element.513, pred[96]{0:T(512)(128)(4,1)S(1)} %get-tuple-element.512), kind=kOutput, calls=%fused_computation.4 | convolution fusion | flops 2419064832 | bytes 18874560 | tf_op jit(solution)/shard_map/while/body/eval_jaxpr/cond/branch_1_fun/pik,pkj->pij/dot_general | solution.py:16
  303.2 6.3 %fusion.8 = f32[24,128,128]{2,0,1:T(8,128)S(1)} fusion(f32[24,128,128]{2,0,1:T(8,128)S(1)} %get-tuple-element.481, f32[96,128,128]{2,1,0:T(8,128)S(1)} %fusion.2, s32[96]{0:T(128)S(1)} %get-tuple-element.514, pred[96]{0:T(512)(128)(4,1)S(1)} %get-tuple-element.511), kind=kOutput, calls=%fused_computation.10 | convolution fusion | flops 453382656 | bytes 9437664 | tf_op jit(solution)/shard_map/while/body/eval_jaxpr/cond/branch_1_fun/op,pij->oij/dot_general | solution.py:21
  309.5 25.6 %conditional.2 = (f32[24,128,128]{2,0,1:T(8,128)S(1)}) conditional(s32[]{:T(128)} %convert_element_type.13, f32[24,128,128]{2,0,1:T(8,128)S(1)} %get-tuple-element.574, (s32[]{:T(128)}, s32[8,96,3]{1,2,0:T(4,128)S(1)}, s32[]{:T(128)}, f32[8,1,16,128,128]{4,3,2,1,0:T(8,128)}, f32[2,4,1,12,128,128]{5,4,3,2,1,0:T(8,128)}, ...), branch_computations={%region_1.1_spmd, %region_2.2_spmd} | conditional | flops 2872450304 | bytes 57163708 | solution.py:42
  309.5 1.2 dynamic-slice_bitcast_fusion.1
  310.8 3.5 gather_fusion.1
  314.3 1.3 dynamic-slice_bitcast_fusion
  315.6 3.6 gather_fusion
  319.2 9.5 %fusion.2 = f32[96,128,128]{2,1,0:T(8,128)S(1)} fusion(f32[96,128,128]{2,1,0:T(8,128)} %gather_fusion.1, f32[96,128,128]{2,1,0:T(8,128)} %gather_fusion, pred[96]{0:T(512)(128)(4,1)S(1)} %get-tuple-element.513, pred[96]{0:T(512)(128)(4,1)S(1)} %get-tuple-element.512), kind=kOutput, calls=%fused_computation.4 | convolution fusion | flops 2419064832 | bytes 18874560 | tf_op jit(solution)/shard_map/while/body/eval_jaxpr/cond/branch_1_fun/pik,pkj->pij/dot_general | solution.py:16
  328.8 6.3 %fusion.8 = f32[24,128,128]{2,0,1:T(8,128)S(1)} fusion(f32[24,128,128]{2,0,1:T(8,128)S(1)} %get-tuple-element.481, f32[96,128,128]{2,1,0:T(8,128)S(1)} %fusion.2, s32[96]{0:T(128)S(1)} %get-tuple-element.514, pred[96]{0:T(512)(128)(4,1)S(1)} %get-tuple-element.511), kind=kOutput, calls=%fused_computation.10 | convolution fusion | flops 453382656 | bytes 9437664 | tf_op jit(solution)/shard_map/while/body/eval_jaxpr/cond/branch_1_fun/op,pij->oij/dot_general | solution.py:21
  335.1 25.6 %conditional.2 = (f32[24,128,128]{2,0,1:T(8,128)S(1)}) conditional(s32[]{:T(128)} %convert_element_type.13, f32[24,128,128]{2,0,1:T(8,128)S(1)} %get-tuple-element.574, (s32[]{:T(128)}, s32[8,96,3]{1,2,0:T(4,128)S(1)}, s32[]{:T(128)}, f32[8,1,16,128,128]{4,3,2,1,0:T(8,128)}, f32[2,4,1,12,128,128]{5,4,3,2,1,0:T(8,128)}, ...), branch_computations={%region_1.1_spmd, %region_2.2_spmd} | conditional | flops 2872450304 | bytes 57163708 | solution.py:42
  335.1 1.2 dynamic-slice_bitcast_fusion.1
  336.4 3.5 gather_fusion.1
  339.9 1.3 dynamic-slice_bitcast_fusion
  341.2 3.6 gather_fusion
  344.8 9.5 %fusion.2 = f32[96,128,128]{2,1,0:T(8,128)S(1)} fusion(f32[96,128,128]{2,1,0:T(8,128)} %gather_fusion.1, f32[96,128,128]{2,1,0:T(8,128)} %gather_fusion, pred[96]{0:T(512)(128)(4,1)S(1)} %get-tuple-element.513, pred[96]{0:T(512)(128)(4,1)S(1)} %get-tuple-element.512), kind=kOutput, calls=%fused_computation.4 | convolution fusion | flops 2419064832 | bytes 18874560 | tf_op jit(solution)/shard_map/while/body/eval_jaxpr/cond/branch_1_fun/pik,pkj->pij/dot_general | solution.py:16
  354.4 6.3 %fusion.8 = f32[24,128,128]{2,0,1:T(8,128)S(1)} fusion(f32[24,128,128]{2,0,1:T(8,128)S(1)} %get-tuple-element.481, f32[96,128,128]{2,1,0:T(8,128)S(1)} %fusion.2, s32[96]{0:T(128)S(1)} %get-tuple-element.514, pred[96]{0:T(512)(128)(4,1)S(1)} %get-tuple-element.511), kind=kOutput, calls=%fused_computation.10 | convolution fusion | flops 453382656 | bytes 9437664 | tf_op jit(solution)/shard_map/while/body/eval_jaxpr/cond/branch_1_fun/op,pij->oij/dot_general | solution.py:21
  360.7 25.6 %conditional.2 = (f32[24,128,128]{2,0,1:T(8,128)S(1)}) conditional(s32[]{:T(128)} %convert_element_type.13, f32[24,128,128]{2,0,1:T(8,128)S(1)} %get-tuple-element.574, (s32[]{:T(128)}, s32[8,96,3]{1,2,0:T(4,128)S(1)}, s32[]{:T(128)}, f32[8,1,16,128,128]{4,3,2,1,0:T(8,128)}, f32[2,4,1,12,128,128]{5,4,3,2,1,0:T(8,128)}, ...), branch_computations={%region_1.1_spmd, %region_2.2_spmd} | conditional | flops 2872450304 | bytes 57163708 | solution.py:42
  360.7 1.2 dynamic-slice_bitcast_fusion.1
  362.0 3.5 gather_fusion.1
  365.5 1.3 dynamic-slice_bitcast_fusion
  366.8 3.6 gather_fusion
  370.4 9.5 %fusion.2 = f32[96,128,128]{2,1,0:T(8,128)S(1)} fusion(f32[96,128,128]{2,1,0:T(8,128)} %gather_fusion.1, f32[96,128,128]{2,1,0:T(8,128)} %gather_fusion, pred[96]{0:T(512)(128)(4,1)S(1)} %get-tuple-element.513, pred[96]{0:T(512)(128)(4,1)S(1)} %get-tuple-element.512), kind=kOutput, calls=%fused_computation.4 | convolution fusion | flops 2419064832 | bytes 18874560 | tf_op jit(solution)/shard_map/while/body/eval_jaxpr/cond/branch_1_fun/pik,pkj->pij/dot_general | solution.py:16
  380.0 6.3 %fusion.8 = f32[24,128,128]{2,0,1:T(8,128)S(1)} fusion(f32[24,128,128]{2,0,1:T(8,128)S(1)} %get-tuple-element.481, f32[96,128,128]{2,1,0:T(8,128)S(1)} %fusion.2, s32[96]{0:T(128)S(1)} %get-tuple-element.514, pred[96]{0:T(512)(128)(4,1)S(1)} %get-tuple-element.511), kind=kOutput, calls=%fused_computation.10 | convolution fusion | flops 453382656 | bytes 9437664 | tf_op jit(solution)/shard_map/while/body/eval_jaxpr/cond/branch_1_fun/op,pij->oij/dot_general | solution.py:21
  386.3 1.4 copy.15
  (34 shorter events, 0.3 us)
Async XLA Ops:
  6.5 120.4 %all-gather.5.cloned.1.call-start = ((), (), s32[]{:S(2)}) async-start(), calls=%async_computation.1 | async-start | bytes 7864320 | tf_op jit(solution)/shard_map/all_gather | solution.py:32
  7.3 174.1 %all-gather.3.cloned.1.call-start = ((), (), s32[]{:S(2)}) async-start(), calls=%async_computation | async-start | bytes 9437184 | tf_op jit(solution)/shard_map/all_gather | solution.py:33
Sparse Core Ops, SparseCore 0:
  8.9 118.0 all-gather.4
  128.9 52.4 all-gather.2
where the time goes:
time: 395 us
  waiting for transfers between devices  174 us (44%)
  matrix products  127 us (32%)
  local copies, waits for them, and re-layouts  79.3 us (20%)
  between operations  13.4 us (3%)
    all_gather x1, waiting for transfers between devices, shards(): right_all = lax.all_gather(right_panels, 'col', axis=1, tiled=True)  118 us
    dot_general x8, matrix products, contribute(): jnp.einsum('pik,pkj->pij', taken_left, taken_right, precision=lax.Precisi...  76.2 us
    all_gather x1, waiting for transfers between devices, shards(): pieces = lax.all_gather(left_panels, 'row', axis=0, tiled=True)  54.4 us
    dot_general x8, matrix products, contribute(): jnp.einsum('op,pij->oij', onehot, blocks, precision=lax.Precision.HIGHEST)  50.3 us
    gather x8, local copies, waits for them, and re-layouts, contribute(): taken_left = jnp.take(left_stack, left_slot, axis=0)  28.9 us
    gather x8, local copies, waits for them, and re-layouts, contribute(): taken_right = jnp.take(right_panel, right_slot, axis=0)  28.2 us
    squeeze x8, local copies, waits for them, and re-layouts, one_row(): left_stack = lax.dynamic_index_in_dim(pieces, offset, 0, keepdims=False)[0]  10.3 us
    squeeze x8, local copies, waits for them, and re-layouts, one_row(): right_panel = right_all[offset // col_count, offset % col_count, 0]  9.53 us
  transfers between devices with their start and end apart: 2, of which 2 were waited for; matrix products, arithmetic and copies ran while one was open for 0% of the time, Pallas kernels for 0%

commit v1 on v0

--- a/solution.py
+++ b/solution.py
@@ -30,7 +30,12 @@
     step_count = entries.shape[0]
     running = jnp.zeros((OCAP, BLK, BLK), jnp.float32)
     right_all = lax.all_gather(right_panels, "col", axis=1, tiled=True)
-    pieces = lax.all_gather(left_panels, "row", axis=0, tiled=True)
+    ring = [left_panels]
+    for hop in range(7):
+        ring.append(lax.ppermute(ring[-1], "row", [(dev, (dev + 1) % 8) for dev in range(8)]))
+    pieces = jnp.roll(
+        jnp.concatenate(ring[::-1], axis=0), (lax.axis_index("row") + 1) * ring[0].shape[0], axis=0
+    )
 
     def one_row(offset, partial_value):
         step_num = (offset - row_pos - col_pos) % row_count

time: 395 us -> 345 us (0.87)
  waiting for transfers between devices: 174 us -> 106 us
  local copies, waits for them, and re-layouts: 79.3 us -> 95.9 us
    all_gather x1, waiting for transfers between devices: 118 us -> 0.01 us  [shards(): right_all = lax.all_gather(right_panels, 'col', axis=1, tiled=True)]
    ppermute x0 -> x7, waiting for transfers between devices: none -> 106 us  [shards(): lax.ppermute(ring[-1], 'row', [(dev, (dev + 1) % 8) for dev in range(8)])]
    all_gather x1 -> x0, waiting for transfers between devices: 54.4 us -> none  [shards(): pieces = lax.all_gather(left_panels, 'row', axis=0, tiled=True)]
    unnamed x1 -> x30, local copies, waits for them, and re-layouts: 0.71 us -> 13.4 us
  transfers between devices with their start and end apart: 2 -> 8, of which waited for: 2 -> 7; matrix products, arithmetic and copies ran while one was open for 0% -> 4% of each run, Pallas kernels for 0% -> 0%
where the time goes in v1:
time: 345 us; the launch traced here: 344 us
  matrix products  127 us (37%)
  waiting for transfers between devices  106 us (31%)
  local copies, waits for them, and re-layouts  95.9 us (28%)
  between operations  13.6 us (4%)
    ppermute x7, waiting for transfers between devices, shards(): lax.ppermute(ring[-1], 'row', [(dev, (dev + 1) % 8) for dev in range(8)])  106 us
    dot_general x8, matrix products, contribute(): jnp.einsum('pik,pkj->pij', taken_left, taken_right, precision=lax.Precisi...  76.2 us
    dot_general x8, matrix products, contribute(): jnp.einsum('op,pij->oij', onehot, blocks, precision=lax.Precision.HIGHEST)  50.3 us
    gather x8, local copies, waits for them, and re-layouts, contribute(): taken_left = jnp.take(left_stack, left_slot, axis=0)  29 us
    gather x8, local copies, waits for them, and re-layouts, contribute(): taken_right = jnp.take(right_panel, right_slot, axis=0)  28.1 us
    unnamed x30, local copies, waits for them, and re-layouts  13.4 us
    squeeze x8, local copies, waits for them, and re-layouts, one_row(): left_stack = lax.dynamic_index_in_dim(pieces, offset, 0, keepdims=False)[0]  10.3 us
    squeeze x8, local copies, waits for them, and re-layouts, one_row(): right_panel = right_all[offset // col_count, offset % col_count, 0]  9.53 us
  transfers between devices with their start and end apart: 8, of which 7 were waited for; matrix products, arithmetic and copies ran while one was open for 4% of the time, Pallas kernels for 0%

profile of v1, /device:TPU:0, one launch (start us, length us, event | category | flops | bytes accessed | tf_op | source)
XLA Modules:
  0.0 344.0 jit_solution(260615498361232686)
XLA Ops:
  7.3 15.4 %collective-permute-done = f32[1,1,16,128,128]{4,3,2,1,0:T(8,128)S(1)} collective-permute-done((f32[1,1,16,128,128]{4,3,2,1,0:T(8,128)}, f32[1,1,16,128,128]{4,3,2,1,0:T(8,128)S(1)}, u32[]{:S(2)}, u32[]{:S(2)}) %collective-permute-start) | collective-permute-done | bytes 1048608 | tf_op jit(solution)/shard_map/ppermute | solution.py:35
  22.7 15.1 %collective-permute-done.1 = f32[1,1,16,128,128]{4,3,2,1,0:T(8,128)S(1)} collective-permute-done((f32[1,1,16,128,128]{4,3,2,1,0:T(8,128)S(1)}, f32[1,1,16,128,128]{4,3,2,1,0:T(8,128)S(1)}, u32[]{:S(2)}, u32[]{:S(2)}) %collective-permute-start.1) | collective-permute-done | bytes 1048608 | tf_op jit(solution)/shard_map/ppermute | solution.py:35
  37.8 15.1 %collective-permute-done.2 = f32[1,1,16,128,128]{4,3,2,1,0:T(8,128)S(1)} collective-permute-done((f32[1,1,16,128,128]{4,3,2,1,0:T(8,128)S(1)}, f32[1,1,16,128,128]{4,3,2,1,0:T(8,128)S(1)}, u32[]{:S(2)}, u32[]{:S(2)}) %collective-permute-start.2) | collective-permute-done | bytes 1048608 | tf_op jit(solution)/shard_map/ppermute | solution.py:35
  53.9 15.1 %collective-permute-done.3 = f32[1,1,16,128,128]{4,3,2,1,0:T(8,128)S(1)} collective-permute-done((f32[1,1,16,128,128]{4,3,2,1,0:T(8,128)S(1)}, f32[1,1,16,128,128]{4,3,2,1,0:T(8,128)S(1)}, u32[]{:S(2)}, u32[]{:S(2)}) %collective-permute-start.3) | collective-permute-done | bytes 1048608 | tf_op jit(solution)/shard_map/ppermute | solution.py:35
  70.0 15.1 %collective-permute-done.4 = f32[1,1,16,128,128]{4,3,2,1,0:T(8,128)S(1)} collective-permute-done((f32[1,1,16,128,128]{4,3,2,1,0:T(8,128)S(1)}, f32[1,1,16,128,128]{4,3,2,1,0:T(8,128)S(1)}, u32[]{:S(2)}, u32[]{:S(2)}) %collective-permute-start.4) | collective-permute-done | bytes 1048608 | tf_op jit(solution)/shard_map/ppermute | solution.py:35
  86.1 15.2 %collective-permute-done.5 = f32[1,1,16,128,128]{4,3,2,1,0:T(8,128)} collective-permute-done((f32[1,1,16,128,128]{4,3,2,1,0:T(8,128)S(1)}, f32[1,1,16,128,128]{4,3,2,1,0:T(8,128)}, u32[]{:S(2)}, u32[]{:S(2)}) %collective-permute-start.5) | collective-permute-done | bytes 1048608 | tf_op jit(solution)/shard_map/ppermute | solution.py:35
  102.1 14.7 %collective-permute-done.6 = f32[1,1,16,128,128]{4,3,2,1,0:T(8,128)} collective-permute-done((f32[1,1,16,128,128]{4,3,2,1,0:T(8,128)}, f32[1,1,16,128,128]{4,3,2,1,0:T(8,128)}, u32[]{:S(2)}, u32[]{:S(2)}) %collective-permute-start.6) | collective-permute-done | bytes 1048608 | tf_op jit(solution)/shard_map/ppermute | solution.py:35
  116.8 1.3 constant_dynamic-update-slice_fusion.15
  118.1 1.3 constant_dynamic-update-slice_fusion.14
  119.4 1.3 constant_dynamic-update-slice_fusion.13
  120.7 1.3 constant_dynamic-update-slice_fusion.12
  122.0 1.3 constant_dynamic-update-slice_fusion.11
  123.6 1.3 constant_dynamic-update-slice_fusion.7
  124.9 1.3 constant_dynamic-update-slice_fusion.6
  126.7 3.8 %constant_dynamic-slice_fusion = f32[8,1,16,128,128]{4,3,2,1,0:T(8,128)} fusion(f32[16,1,16,128,128]{4,3,2,1,0:T(8,128)S(1)} %constant_dynamic-update-slice_fusion, s32[]{:T(128)S(6)} %select_n.149), kind=kLoop, calls=%fused_computation.47 | loop fusion | bytes 16777220 | tf_op jit(solution)/shard_map/jit(_roll_dynamic)/dynamic_slice | solution.py:36
  130.7 205.0 %while.19 = (s32[]{:T(128)}, f32[24,128,128]{2,0,1:T(8,128)S(1)}, s32[]{:T(128)}, s32[]{:T(128)}, s32[8,96,3]{1,2,0:T(4,128)S(1)}, /*index=5*/f32[8,1,16,128,128...) while((s32[]{:T(128)}, f32[24,128,128]{2,0,1:T(8,128)S(1)}, ...), condition=%wide.region_3.4_spmd, body=%wide.region_0.3_spmd.sunk | while | flops 2872450304 | bytes 57164012 | solution.py:54
  130.9 25.6 %conditional.2 = (f32[24,128,128]{2,0,1:T(8,128)S(1)}) conditional(s32[]{:T(128)} %convert_element_type.13, f32[24,128,128]{2,0,1:T(8,128)S(1)} %get-tuple-element.574, (s32[]{:T(128)}, s32[8,96,3]{1,2,0:T(4,128)S(1)}, s32[]{:T(128)}, f32[8,1,16,128,128]{4,3,2,1,0:T(8,128)}, f32[2,4,1,12,128,128]{5,4,3,2,1,0:T(8,128)}, ...), branch_computations={%region_1.1_spmd, %region_2.2_spmd} | conditional | flops 2872450304 | bytes 57163708 | solution.py:47
  132.2 3.5 %gather_fusion.1 = f32[96,128,128]{2,1,0:T(8,128)} fusion(f32[12,128,128]{2,1,0:T(8,128)S(1)} %dynamic-slice_bitcast_fusion.1, s32[1024]{0:T(1024)S(1)} %get-tuple-element.517), kind=kCustom, calls=%fused_computation.1 | custom fusion | bytes 12583296 | tf_op jit(solution)/shard_map/while/body/eval_jaxpr/cond/branch_1_fun/jit(_take)/gather | solution.py:15
  135.7 1.3 dynamic-slice_bitcast_fusion
  137.0 3.6 %gather_fusion = f32[96,128,128]{2,1,0:T(8,128)} fusion(f32[16,128,128]{2,1,0:T(8,128)S(1)} %dynamic-slice_bitcast_fusion, s32[1024]{0:T(1024)S(1)} %get-tuple-element.518), kind=kCustom, calls=%fused_computation | custom fusion | bytes 12583296 | tf_op jit(solution)/shard_map/while/body/eval_jaxpr/cond/branch_1_fun/jit(_take)/gather | solution.py:14
  140.6 9.5 %fusion.2 = f32[96,128,128]{2,1,0:T(8,128)S(1)} fusion(f32[96,128,128]{2,1,0:T(8,128)} %gather_fusion.1, f32[96,128,128]{2,1,0:T(8,128)} %gather_fusion, pred[96]{0:T(512)(128)(4,1)S(1)} %get-tuple-element.513, pred[96]{0:T(512)(128)(4,1)S(1)} %get-tuple-element.512), kind=kOutput, calls=%fused_computation.4 | convolution fusion | flops 2419064832 | bytes 18874560 | tf_op jit(solution)/shard_map/while/body/eval_jaxpr/cond/branch_1_fun/pik,pkj->pij/dot_general | solution.py:16
  150.2 6.3 %fusion.8 = f32[24,128,128]{2,0,1:T(8,128)S(1)} fusion(f32[24,128,128]{2,0,1:T(8,128)S(1)} %get-tuple-element.481, f32[96,128,128]{2,1,0:T(8,128)S(1)} %fusion.2, s32[96]{0:T(128)S(1)} %get-tuple-element.514, pred[96]{0:T(512)(128)(4,1)S(1)} %get-tuple-element.511), kind=kOutput, calls=%fused_computation.10 | convolution fusion | flops 453382656 | bytes 9437664 | tf_op jit(solution)/shard_map/while/body/eval_jaxpr/cond/branch_1_fun/op,pij->oij/dot_general | solution.py:21
  156.5 25.6 %conditional.2 = (f32[24,128,128]{2,0,1:T(8,128)S(1)}) conditional(s32[]{:T(128)} %convert_element_type.13, f32[24,128,128]{2,0,1:T(8,128)S(1)} %get-tuple-element.574, (s32[]{:T(128)}, s32[8,96,3]{1,2,0:T(4,128)S(1)}, s32[]{:T(128)}, f32[8,1,16,128,128]{4,3,2,1,0:T(8,128)}, f32[2,4,1,12,128,128]{5,4,3,2,1,0:T(8,128)}, ...), branch_computations={%region_1.1_spmd, %region_2.2_spmd} | conditional | flops 2872450304 | bytes 57163708 | solution.py:47
  157.8 3.5 %gather_fusion.1 = f32[96,128,128]{2,1,0:T(8,128)} fusion(f32[12,128,128]{2,1,0:T(8,128)S(1)} %dynamic-slice_bitcast_fusion.1, s32[1024]{0:T(1024)S(1)} %get-tuple-element.517), kind=kCustom, calls=%fused_computation.1 | custom fusion | bytes 12583296 | tf_op jit(solution)/shard_map/while/body/eval_jaxpr/cond/branch_1_fun/jit(_take)/gather | solution.py:15
  161.3 1.3 dynamic-slice_bitcast_fusion
  162.6 3.6 %gather_fusion = f32[96,128,128]{2,1,0:T(8,128)} fusion(f32[16,128,128]{2,1,0:T(8,128)S(1)} %dynamic-slice_bitcast_fusion, s32[1024]{0:T(1024)S(1)} %get-tuple-element.518), kind=kCustom, calls=%fused_computation | custom fusion | bytes 12583296 | tf_op jit(solution)/shard_map/while/body/eval_jaxpr/cond/branch_1_fun/jit(_take)/gather | solution.py:14
  166.2 9.5 %fusion.2 = f32[96,128,128]{2,1,0:T(8,128)S(1)} fusion(f32[96,128,128]{2,1,0:T(8,128)} %gather_fusion.1, f32[96,128,128]{2,1,0:T(8,128)} %gather_fusion, pred[96]{0:T(512)(128)(4,1)S(1)} %get-tuple-element.513, pred[96]{0:T(512)(128)(4,1)S(1)} %get-tuple-element.512), kind=kOutput, calls=%fused_computation.4 | convolution fusion | flops 2419064832 | bytes 18874560 | tf_op jit(solution)/shard_map/while/body/eval_jaxpr/cond/branch_1_fun/pik,pkj->pij/dot_general | solution.py:16
  175.8 6.3 %fusion.8 = f32[24,128,128]{2,0,1:T(8,128)S(1)} fusion(f32[24,128,128]{2,0,1:T(8,128)S(1)} %get-tuple-element.481, f32[96,128,128]{2,1,0:T(8,128)S(1)} %fusion.2, s32[96]{0:T(128)S(1)} %get-tuple-element.514, pred[96]{0:T(512)(128)(4,1)S(1)} %get-tuple-element.511), kind=kOutput, calls=%fused_computation.10 | convolution fusion | flops 453382656 | bytes 9437664 | tf_op jit(solution)/shard_map/while/body/eval_jaxpr/cond/branch_1_fun/op,pij->oij/dot_general | solution.py:21
  182.1 25.6 %conditional.2 = (f32[24,128,128]{2,0,1:T(8,128)S(1)}) conditional(s32[]{:T(128)} %convert_element_type.13, f32[24,128,128]{2,0,1:T(8,128)S(1)} %get-tuple-element.574, (s32[]{:T(128)}, s32[8,96,3]{1,2,0:T(4,128)S(1)}, s32[]{:T(128)}, f32[8,1,16,128,128]{4,3,2,1,0:T(8,128)}, f32[2,4,1,12,128,128]{5,4,3,2,1,0:T(8,128)}, ...), branch_computations={%region_1.1_spmd, %region_2.2_spmd} | conditional | flops 2872450304 | bytes 57163708 | solution.py:47
  183.4 3.5 %gather_fusion.1 = f32[96,128,128]{2,1,0:T(8,128)} fusion(f32[12,128,128]{2,1,0:T(8,128)S(1)} %dynamic-slice_bitcast_fusion.1, s32[1024]{0:T(1024)S(1)} %get-tuple-element.517), kind=kCustom, calls=%fused_computation.1 | custom fusion | bytes 12583296 | tf_op jit(solution)/shard_map/while/body/eval_jaxpr/cond/branch_1_fun/jit(_take)/gather | solution.py:15
  186.9 1.3 dynamic-slice_bitcast_fusion
  188.2 3.6 %gather_fusion = f32[96,128,128]{2,1,0:T(8,128)} fusion(f32[16,128,128]{2,1,0:T(8,128)S(1)} %dynamic-slice_bitcast_fusion, s32[1024]{0:T(1024)S(1)} %get-tuple-element.518), kind=kCustom, calls=%fused_computation | custom fusion | bytes 12583296 | tf_op jit(solution)/shard_map/while/body/eval_jaxpr/cond/branch_1_fun/jit(_take)/gather | solution.py:14
  191.8 9.5 %fusion.2 = f32[96,128,128]{2,1,0:T(8,128)S(1)} fusion(f32[96,128,128]{2,1,0:T(8,128)} %gather_fusion.1, f32[96,128,128]{2,1,0:T(8,128)} %gather_fusion, pred[96]{0:T(512)(128)(4,1)S(1)} %get-tuple-element.513, pred[96]{0:T(512)(128)(4,1)S(1)} %get-tuple-element.512), kind=kOutput, calls=%fused_computation.4 | convolution fusion | flops 2419064832 | bytes 18874560 | tf_op jit(solution)/shard_map/while/body/eval_jaxpr/cond/branch_1_fun/pik,pkj->pij/dot_general | solution.py:16
  201.4 6.3 %fusion.8 = f32[24,128,128]{2,0,1:T(8,128)S(1)} fusion(f32[24,128,128]{2,0,1:T(8,128)S(1)} %get-tuple-element.481, f32[96,128,128]{2,1,0:T(8,128)S(1)} %fusion.2, s32[96]{0:T(128)S(1)} %get-tuple-element.514, pred[96]{0:T(512)(128)(4,1)S(1)} %get-tuple-element.511), kind=kOutput, calls=%fused_computation.10 | convolution fusion | flops 453382656 | bytes 9437664 | tf_op jit(solution)/shard_map/while/body/eval_jaxpr/cond/branch_1_fun/op,pij->oij/dot_general | solution.py:21
  207.7 25.6 %conditional.2 = (f32[24,128,128]{2,0,1:T(8,128)S(1)}) conditional(s32[]{:T(128)} %convert_element_type.13, f32[24,128,128]{2,0,1:T(8,128)S(1)} %get-tuple-element.574, (s32[]{:T(128)}, s32[8,96,3]{1,2,0:T(4,128)S(1)}, s32[]{:T(128)}, f32[8,1,16,128,128]{4,3,2,1,0:T(8,128)}, f32[2,4,1,12,128,128]{5,4,3,2,1,0:T(8,128)}, ...), branch_computations={%region_1.1_spmd, %region_2.2_spmd} | conditional | flops 2872450304 | bytes 57163708 | solution.py:47
  209.0 3.5 %gather_fusion.1 = f32[96,128,128]{2,1,0:T(8,128)} fusion(f32[12,128,128]{2,1,0:T(8,128)S(1)} %dynamic-slice_bitcast_fusion.1, s32[1024]{0:T(1024)S(1)} %get-tuple-element.517), kind=kCustom, calls=%fused_computation.1 | custom fusion | bytes 12583296 | tf_op jit(solution)/shard_map/while/body/eval_jaxpr/cond/branch_1_fun/jit(_take)/gather | solution.py:15
  212.5 1.3 dynamic-slice_bitcast_fusion
  213.8 3.6 %gather_fusion = f32[96,128,128]{2,1,0:T(8,128)} fusion(f32[16,128,128]{2,1,0:T(8,128)S(1)} %dynamic-slice_bitcast_fusion, s32[1024]{0:T(1024)S(1)} %get-tuple-element.518), kind=kCustom, calls=%fused_computation | custom fusion | bytes 12583296 | tf_op jit(solution)/shard_map/while/body/eval_jaxpr/cond/branch_1_fun/jit(_take)/gather | solution.py:14
  217.4 9.5 %fusion.2 = f32[96,128,128]{2,1,0:T(8,128)S(1)} fusion(f32[96,128,128]{2,1,0:T(8,128)} %gather_fusion.1, f32[96,128,128]{2,1,0:T(8,128)} %gather_fusion, pred[96]{0:T(512)(128)(4,1)S(1)} %get-tuple-element.513, pred[96]{0:T(512)(128)(4,1)S(1)} %get-tuple-element.512), kind=kOutput, calls=%fused_computation.4 | convolution fusion | flops 2419064832 | bytes 18874560 | tf_op jit(solution)/shard_map/while/body/eval_jaxpr/cond/branch_1_fun/pik,pkj->pij/dot_general | solution.py:16
  227.0 6.3 %fusion.8 = f32[24,128,128]{2,0,1:T(8,128)S(1)} fusion(f32[24,128,128]{2,0,1:T(8,128)S(1)} %get-tuple-element.481, f32[96,128,128]{2,1,0:T(8,128)S(1)} %fusion.2, s32[96]{0:T(128)S(1)} %get-tuple-element.514, pred[96]{0:T(512)(128)(4,1)S(1)} %get-tuple-element.511), kind=kOutput, calls=%fused_computation.10 | convolution fusion | flops 453382656 | bytes 9437664 | tf_op jit(solution)/shard_map/while/body/eval_jaxpr/cond/branch_1_fun/op,pij->oij/dot_general | solution.py:21
  233.3 25.6 %conditional.2 = (f32[24,128,128]{2,0,1:T(8,128)S(1)}) conditional(s32[]{:T(128)} %convert_element_type.13, f32[24,128,128]{2,0,1:T(8,128)S(1)} %get-tuple-element.574, (s32[]{:T(128)}, s32[8,96,3]{1,2,0:T(4,128)S(1)}, s32[]{:T(128)}, f32[8,1,16,128,128]{4,3,2,1,0:T(8,128)}, f32[2,4,1,12,128,128]{5,4,3,2,1,0:T(8,128)}, ...), branch_computations={%region_1.1_spmd, %region_2.2_spmd} | conditional | flops 2872450304 | bytes 57163708 | solution.py:47
  234.6 3.5 %gather_fusion.1 = f32[96,128,128]{2,1,0:T(8,128)} fusion(f32[12,128,128]{2,1,0:T(8,128)S(1)} %dynamic-slice_bitcast_fusion.1, s32[1024]{0:T(1024)S(1)} %get-tuple-element.517), kind=kCustom, calls=%fused_computation.1 | custom fusion | bytes 12583296 | tf_op jit(solution)/shard_map/while/body/eval_jaxpr/cond/branch_1_fun/jit(_take)/gather | solution.py:15
  238.1 1.3 dynamic-slice_bitcast_fusion
  239.4 3.6 %gather_fusion = f32[96,128,128]{2,1,0:T(8,128)} fusion(f32[16,128,128]{2,1,0:T(8,128)S(1)} %dynamic-slice_bitcast_fusion, s32[1024]{0:T(1024)S(1)} %get-tuple-element.518), kind=kCustom, calls=%fused_computation | custom fusion | bytes 12583296 | tf_op jit(solution)/shard_map/while/body/eval_jaxpr/cond/branch_1_fun/jit(_take)/gather | solution.py:14
  243.0 9.5 %fusion.2 = f32[96,128,128]{2,1,0:T(8,128)S(1)} fusion(f32[96,128,128]{2,1,0:T(8,128)} %gather_fusion.1, f32[96,128,128]{2,1,0:T(8,128)} %gather_fusion, pred[96]{0:T(512)(128)(4,1)S(1)} %get-tuple-element.513, pred[96]{0:T(512)(128)(4,1)S(1)} %get-tuple-element.512), kind=kOutput, calls=%fused_computation.4 | convolution fusion | flops 2419064832 | bytes 18874560 | tf_op jit(solution)/shard_map/while/body/eval_jaxpr/cond/branch_1_fun/pik,pkj->pij/dot_general | solution.py:16
  252.6 6.3 %fusion.8 = f32[24,128,128]{2,0,1:T(8,128)S(1)} fusion(f32[24,128,128]{2,0,1:T(8,128)S(1)} %get-tuple-element.481, f32[96,128,128]{2,1,0:T(8,128)S(1)} %fusion.2, s32[96]{0:T(128)S(1)} %get-tuple-element.514, pred[96]{0:T(512)(128)(4,1)S(1)} %get-tuple-element.511), kind=kOutput, calls=%fused_computation.10 | convolution fusion | flops 453382656 | bytes 9437664 | tf_op jit(solution)/shard_map/while/body/eval_jaxpr/cond/branch_1_fun/op,pij->oij/dot_general | solution.py:21
  258.9 25.6 %conditional.2 = (f32[24,128,128]{2,0,1:T(8,128)S(1)}) conditional(s32[]{:T(128)} %convert_element_type.13, f32[24,128,128]{2,0,1:T(8,128)S(1)} %get-tuple-element.574, (s32[]{:T(128)}, s32[8,96,3]{1,2,0:T(4,128)S(1)}, s32[]{:T(128)}, f32[8,1,16,128,128]{4,3,2,1,0:T(8,128)}, f32[2,4,1,12,128,128]{5,4,3,2,1,0:T(8,128)}, ...), branch_computations={%region_1.1_spmd, %region_2.2_spmd} | conditional | flops 2872450304 | bytes 57163708 | solution.py:47
  260.2 3.5 %gather_fusion.1 = f32[96,128,128]{2,1,0:T(8,128)} fusion(f32[12,128,128]{2,1,0:T(8,128)S(1)} %dynamic-slice_bitcast_fusion.1, s32[1024]{0:T(1024)S(1)} %get-tuple-element.517), kind=kCustom, calls=%fused_computation.1 | custom fusion | bytes 12583296 | tf_op jit(solution)/shard_map/while/body/eval_jaxpr/cond/branch_1_fun/jit(_take)/gather | solution.py:15
  263.7 1.3 dynamic-slice_bitcast_fusion
  265.0 3.6 %gather_fusion = f32[96,128,128]{2,1,0:T(8,128)} fusion(f32[16,128,128]{2,1,0:T(8,128)S(1)} %dynamic-slice_bitcast_fusion, s32[1024]{0:T(1024)S(1)} %get-tuple-element.518), kind=kCustom, calls=%fused_computation | custom fusion | bytes 12583296 | tf_op jit(solution)/shard_map/while/body/eval_jaxpr/cond/branch_1_fun/jit(_take)/gather | solution.py:14
  268.6 9.5 %fusion.2 = f32[96,128,128]{2,1,0:T(8,128)S(1)} fusion(f32[96,128,128]{2,1,0:T(8,128)} %gather_fusion.1, f32[96,128,128]{2,1,0:T(8,128)} %gather_fusion, pred[96]{0:T(512)(128)(4,1)S(1)} %get-tuple-element.513, pred[96]{0:T(512)(128)(4,1)S(1)} %get-tuple-element.512), kind=kOutput, calls=%fused_computation.4 | convolution fusion | flops 2419064832 | bytes 18874560 | tf_op jit(solution)/shard_map/while/body/eval_jaxpr/cond/branch_1_fun/pik,pkj->pij/dot_general | solution.py:16
  278.2 6.3 %fusion.8 = f32[24,128,128]{2,0,1:T(8,128)S(1)} fusion(f32[24,128,128]{2,0,1:T(8,128)S(1)} %get-tuple-element.481, f32[96,128,128]{2,1,0:T(8,128)S(1)} %fusion.2, s32[96]{0:T(128)S(1)} %get-tuple-element.514, pred[96]{0:T(512)(128)(4,1)S(1)} %get-tuple-element.511), kind=kOutput, calls=%fused_computation.10 | convolution fusion | flops 453382656 | bytes 9437664 | tf_op jit(solution)/shard_map/while/body/eval_jaxpr/cond/branch_1_fun/op,pij->oij/dot_general | solution.py:21
  284.5 25.6 %conditional.2 = (f32[24,128,128]{2,0,1:T(8,128)S(1)}) conditional(s32[]{:T(128)} %convert_element_type.13, f32[24,128,128]{2,0,1:T(8,128)S(1)} %get-tuple-element.574, (s32[]{:T(128)}, s32[8,96,3]{1,2,0:T(4,128)S(1)}, s32[]{:T(128)}, f32[8,1,16,128,128]{4,3,2,1,0:T(8,128)}, f32[2,4,1,12,128,128]{5,4,3,2,1,0:T(8,128)}, ...), branch_computations={%region_1.1_spmd, %region_2.2_spmd} | conditional | flops 2872450304 | bytes 57163708 | solution.py:47
  285.8 3.5 %gather_fusion.1 = f32[96,128,128]{2,1,0:T(8,128)} fusion(f32[12,128,128]{2,1,0:T(8,128)S(1)} %dynamic-slice_bitcast_fusion.1, s32[1024]{0:T(1024)S(1)} %get-tuple-element.517), kind=kCustom, calls=%fused_computation.1 | custom fusion | bytes 12583296 | tf_op jit(solution)/shard_map/while/body/eval_jaxpr/cond/branch_1_fun/jit(_take)/gather | solution.py:15
  290.6 3.6 %gather_fusion = f32[96,128,128]{2,1,0:T(8,128)} fusion(f32[16,128,128]{2,1,0:T(8,128)S(1)} %dynamic-slice_bitcast_fusion, s32[1024]{0:T(1024)S(1)} %get-tuple-element.518), kind=kCustom, calls=%fused_computation | custom fusion | bytes 12583296 | tf_op jit(solution)/shard_map/while/body/eval_jaxpr/cond/branch_1_fun/jit(_take)/gather | solution.py:14
  294.2 9.5 %fusion.2 = f32[96,128,128]{2,1,0:T(8,128)S(1)} fusion(f32[96,128,128]{2,1,0:T(8,128)} %gather_fusion.1, f32[96,128,128]{2,1,0:T(8,128)} %gather_fusion, pred[96]{0:T(512)(128)(4,1)S(1)} %get-tuple-element.513, pred[96]{0:T(512)(128)(4,1)S(1)} %get-tuple-element.512), kind=kOutput, calls=%fused_computation.4 | convolution fusion | flops 2419064832 | bytes 18874560 | tf_op jit(solution)/shard_map/while/body/eval_jaxpr/cond/branch_1_fun/pik,pkj->pij/dot_general | solution.py:16
  303.8 6.3 %fusion.8 = f32[24,128,128]{2,0,1:T(8,128)S(1)} fusion(f32[24,128,128]{2,0,1:T(8,128)S(1)} %get-tuple-element.481, f32[96,128,128]{2,1,0:T(8,128)S(1)} %fusion.2, s32[96]{0:T(128)S(1)} %get-tuple-element.514, pred[96]{0:T(512)(128)(4,1)S(1)} %get-tuple-element.511), kind=kOutput, calls=%fused_computation.10 | convolution fusion | flops 453382656 | bytes 9437664 | tf_op jit(solution)/shard_map/while/body/eval_jaxpr/cond/branch_1_fun/op,pij->oij/dot_general | solution.py:21
  310.1 25.6 %conditional.2 = (f32[24,128,128]{2,0,1:T(8,128)S(1)}) conditional(s32[]{:T(128)} %convert_element_type.13, f32[24,128,128]{2,0,1:T(8,128)S(1)} %get-tuple-element.574, (s32[]{:T(128)}, s32[8,96,3]{1,2,0:T(4,128)S(1)}, s32[]{:T(128)}, f32[8,1,16,128,128]{4,3,2,1,0:T(8,128)}, f32[2,4,1,12,128,128]{5,4,3,2,1,0:T(8,128)}, ...), branch_computations={%region_1.1_spmd, %region_2.2_spmd} | conditional | flops 2872450304 | bytes 57163708 | solution.py:47
  311.4 3.5 %gather_fusion.1 = f32[96,128,128]{2,1,0:T(8,128)} fusion(f32[12,128,128]{2,1,0:T(8,128)S(1)} %dynamic-slice_bitcast_fusion.1, s32[1024]{0:T(1024)S(1)} %get-tuple-element.517), kind=kCustom, calls=%fused_computation.1 | custom fusion | bytes 12583296 | tf_op jit(solution)/shard_map/while/body/eval_jaxpr/cond/branch_1_fun/jit(_take)/gather | solution.py:15
  314.9 1.3 dynamic-slice_bitcast_fusion
  316.2 3.6 %gather_fusion = f32[96,128,128]{2,1,0:T(8,128)} fusion(f32[16,128,128]{2,1,0:T(8,128)S(1)} %dynamic-slice_bitcast_fusion, s32[1024]{0:T(1024)S(1)} %get-tuple-element.518), kind=kCustom, calls=%fused_computation | custom fusion | bytes 12583296 | tf_op jit(solution)/shard_map/while/body/eval_jaxpr/cond/branch_1_fun/jit(_take)/gather | solution.py:14
  319.8 9.5 %fusion.2 = f32[96,128,128]{2,1,0:T(8,128)S(1)} fusion(f32[96,128,128]{2,1,0:T(8,128)} %gather_fusion.1, f32[96,128,128]{2,1,0:T(8,128)} %gather_fusion, pred[96]{0:T(512)(128)(4,1)S(1)} %get-tuple-element.513, pred[96]{0:T(512)(128)(4,1)S(1)} %get-tuple-element.512), kind=kOutput, calls=%fused_computation.4 | convolution fusion | flops 2419064832 | bytes 18874560 | tf_op jit(solution)/shard_map/while/body/eval_jaxpr/cond/branch_1_fun/pik,pkj->pij/dot_general | solution.py:16
  329.4 6.3 %fusion.8 = f32[24,128,128]{2,0,1:T(8,128)S(1)} fusion(f32[24,128,128]{2,0,1:T(8,128)S(1)} %get-tuple-element.481, f32[96,128,128]{2,1,0:T(8,128)S(1)} %fusion.2, s32[96]{0:T(128)S(1)} %get-tuple-element.514, pred[96]{0:T(512)(128)(4,1)S(1)} %get-tuple-element.511), kind=kOutput, calls=%fused_computation.10 | convolution fusion | flops 453382656 | bytes 9437664 | tf_op jit(solution)/shard_map/while/body/eval_jaxpr/cond/branch_1_fun/op,pij->oij/dot_general | solution.py:21
  335.7 1.4 copy.13
  (76 shorter events, 16.3 us)
Async XLA Ops:
  6.5 116.9 %copy-start = (f32[1,1,16,128,128]{4,3,2,1,0:T(8,128)S(1)}, f32[1,1,16,128,128]{4,3,2,1,0:T(8,128)}, u32[]{:S(2)}) copy-start(f32[1,1,16,128,128]{4,3,2,1,0:T(8,128)} %param.7) | copy-start | bytes 3145732
  6.5 124.0 %all-gather.2.cloned.1.call-start = ((), (), s32[]{:S(2)}) async-start(), calls=%async_computation | async-start | bytes 7864320 | tf_op jit(solution)/shard_map/all_gather | solution.py:32
  6.5 16.1 %collective-permute-start = (f32[1,1,16,128,128]{4,3,2,1,0:T(8,128)}, f32[1,1,16,128,128]{4,3,2,1,0:T(8,128)S(1)}, u32[]{:S(2)}, u32[]{:S(2)}) collective-permute-start(f32[1,1,16,128,128]{4,3,2,1,0:T(8,128)} %param.7), channel_id=1, source_target_pairs={{0,4},{4,8},{8,12},{12,16},{16,20},{20,24},{24,28},{28,0},{1,5},{5... | collective-permute-start | bytes 3145736 | tf_op jit(solution)/shard_map/ppermute | solution.py:35
  22.7 15.1 %collective-permute-start.1 = (f32[1,1,16,128,128]{4,3,2,1,0:T(8,128)S(1)}, f32[1,1,16,128,128]{4,3,2,1,0:T(8,128)S(1)}, u32[]{:S(2)}, u32[]{:S(2)}) collective-permute-start(f32[1,1,16,128,128]{4,3,2,1,0:T(8,128)S(1)} %collective-permute-done), channel_id=1, source_target_pairs={{0,4},{4,8},{8,12},{12,16},{16,20},{20,24},{24,28},{28,0},{1,5},{5... | collective-permute-start | bytes 3145736 | tf_op jit(solution)/shard_map/ppermute | solution.py:35
  37.8 15.1 %collective-permute-start.2 = (f32[1,1,16,128,128]{4,3,2,1,0:T(8,128)S(1)}, f32[1,1,16,128,128]{4,3,2,1,0:T(8,128)S(1)}, u32[]{:S(2)}, u32[]{:S(2)}) collective-permute-start(f32[1,1,16,128,128]{4,3,2,1,0:T(8,128)S(1)} %collective-permute-done.1), channel_id=1, source_target_pairs={{0,4},{4,8},{8,12},{12,16},{16,20},{20,24},{24,28},{28,0},{1,5},{5... | collective-permute-start | bytes 3145736 | tf_op jit(solution)/shard_map/ppermute | solution.py:35
  52.9 1.0 copy-start.1
  53.9 15.1 %collective-permute-start.3 = (f32[1,1,16,128,128]{4,3,2,1,0:T(8,128)S(1)}, f32[1,1,16,128,128]{4,3,2,1,0:T(8,128)S(1)}, u32[]{:S(2)}, u32[]{:S(2)}) collective-permute-start(f32[1,1,16,128,128]{4,3,2,1,0:T(8,128)S(1)} %collective-permute-done.2), channel_id=1, source_target_pairs={{0,4},{4,8},{8,12},{12,16},{16,20},{20,24},{24,28},{28,0},{1,5},{5... | collective-permute-start | bytes 3145736 | tf_op jit(solution)/shard_map/ppermute | solution.py:35
  69.0 1.0 copy-start.3
  70.0 15.1 %collective-permute-start.4 = (f32[1,1,16,128,128]{4,3,2,1,0:T(8,128)S(1)}, f32[1,1,16,128,128]{4,3,2,1,0:T(8,128)S(1)}, u32[]{:S(2)}, u32[]{:S(2)}) collective-permute-start(f32[1,1,16,128,128]{4,3,2,1,0:T(8,128)S(1)} %collective-permute-done.3), channel_id=1, source_target_pairs={{0,4},{4,8},{8,12},{12,16},{16,20},{20,24},{24,28},{28,0},{1,5},{5... | collective-permute-start | bytes 3145736 | tf_op jit(solution)/shard_map/ppermute | solution.py:35
  85.1 1.0 copy-start.5
  86.1 15.2 %collective-permute-start.5 = (f32[1,1,16,128,128]{4,3,2,1,0:T(8,128)S(1)}, f32[1,1,16,128,128]{4,3,2,1,0:T(8,128)}, u32[]{:S(2)}, u32[]{:S(2)}) collective-permute-start(f32[1,1,16,128,128]{4,3,2,1,0:T(8,128)S(1)} %collective-permute-done.4), channel_id=1, source_target_pairs={{0,4},{4,8},{8,12},{12,16},{16,20},{20,24},{24,28},{28,0},{1,5},{5... | collective-permute-start | bytes 3145736 | tf_op jit(solution)/shard_map/ppermute | solution.py:35
  101.3 15.4 %collective-permute-start.6 = (f32[1,1,16,128,128]{4,3,2,1,0:T(8,128)}, f32[1,1,16,128,128]{4,3,2,1,0:T(8,128)}, u32[]{:S(2)}, u32[]{:S(2)}) collective-permute-start(f32[1,1,16,128,128]{4,3,2,1,0:T(8,128)} %collective-permute-done.5), channel_id=1, source_target_pairs={{0,4},{4,8},{8,12},{12,16},{16,20},{20,24},{24,28},{28,0},{1,5},{5... | collective-permute-start | bytes 3145736 | tf_op jit(solution)/shard_map/ppermute | solution.py:35
  102.0 24.1 %copy-start.6 = (f32[1,1,16,128,128]{4,3,2,1,0:T(8,128)S(1)}, f32[1,1,16,128,128]{4,3,2,1,0:T(8,128)}, u32[]{:S(2)}) copy-start(f32[1,1,16,128,128]{4,3,2,1,0:T(8,128)} %copy-done.5) | copy-start | bytes 3145732
  102.0 24.2 %copy-start.4 = (f32[1,1,16,128,128]{4,3,2,1,0:T(8,128)S(1)}, f32[1,1,16,128,128]{4,3,2,1,0:T(8,128)}, u32[]{:S(2)}) copy-start(f32[1,1,16,128,128]{4,3,2,1,0:T(8,128)} %copy-done.3) | copy-start | bytes 3145732
  102.1 24.3 %copy-start.2 = (f32[1,1,16,128,128]{4,3,2,1,0:T(8,128)S(1)}, f32[1,1,16,128,128]{4,3,2,1,0:T(8,128)}, u32[]{:S(2)}) copy-start(f32[1,1,16,128,128]{4,3,2,1,0:T(8,128)} %copy-done.1) | copy-start | bytes 3145732
Sparse Core Ops, SparseCore 0:
  8.9 118.0 all-gather.1
